TPU v7x, 256 devices: a whole 4x4x8 slice. The times are simulated.
256 devices in a mesh: replica: 16 (over y_lo, x, core), shard: 16 (over y_hi, z).
Axes of the slice: x: 4, y: 4 (y_hi: 2, y_lo: 2; y = y_hi * 2 + y_lo), z: 8, core: 2. Of those that a mesh axis runs over, the one named last changes fastest.
Arguments:
- grads: bfloat16 [16, 16, 256, 8192], P('replica', 'shard'), may hold values from -1.25 to 1.25
- master: float32 [256, 8192], P('shard'), may hold values from -0.003 to 0.003
- moment_one: float32 [256, 8192], P('shard'), may hold values from -0.75 to 0.75
- moment_two: float32 [256, 8192], P('shard'), may hold values from 0.005 to 0.2
Outputs:
- master_out: float32 [256, 8192], P('shard')
- moment_one_out: float32 [256, 8192], P('shard')
- moment_two_out: float32 [256, 8192], P('shard')
- weights: bfloat16 [256, 8192], replicated
All inputs are finite; a program needn't handle non-finite values.
Results may differ from a plain program's by a relative error of at most 0.012.
Values may be sent and summed in bfloat16 or wider, within the bound.
No kernel may reach another device: no remote copies, remote signals or barrier semaphores. Data moves between devices by JAX's collectives and lax.ppermute only.
A program may use at most 64 MiB of HBM per device.

v0:
```python
import jax
import jax.numpy as jnp
from jax import lax
from jax.sharding import PartitionSpec as P

STEP = 20


def adam_update(total, master, moment_one, moment_two):
    first = 0.9 * moment_one + 0.1 * total
    second = 0.95 * moment_two + 0.05 * total * total
    first_hat = first / (1.0 - 0.9**STEP)
    second_hat = second / (1.0 - 0.95**STEP)
    updated = master - 0.0003 * (first_hat / (jnp.sqrt(second_hat) + 1e-08) + 0.1 * master)
    return (updated, first, second)


def local(grads, master, moment_one, moment_two):
    local_grad = grads[0, 0]
    group_sum = lax.psum_scatter(
        local_grad.astype(jnp.float32).astype(jnp.bfloat16),
        "shard",
        scatter_dimension=0,
        tiled=True,
    ).astype(jnp.float32)
    total = lax.psum(group_sum, "replica")
    updated, first, second = adam_update(total, master, moment_one, moment_two)
    weights = lax.all_gather(updated.astype(jnp.bfloat16), "shard", axis=0, tiled=True)
    return (updated, first, second, weights)


def solution(mesh):
    placed = (
        P("replica", "shard", None, None),
        P("shard", None),
        P("shard", None),
        P("shard", None),
    )
    return jax.shard_map(
        local,
        mesh=mesh,
        in_specs=placed,
        out_specs=(P("shard", None), P("shard", None), P("shard", None), P()),
        check_vma=False,
    )
```

profile of v0, /device:TPU:2, one launch (start us, length us, event | category | flops | bytes accessed | tf_op | source)
XLA Modules:
  0.0 396.3 jit_solution(3998188347045665005)
XLA Ops:
  7.2 0.0 copy-start.2
  7.2 0.0 copy-start.1
  7.2 0.0 copy-start
  7.2 0.0 reduce-scatter.2.cloned.1.call-start
  7.2 0.7 reduce-scatter.2.cloned.1.call-update
  7.9 0.0 all-gather.2.cloned.1.call-start
  8.0 221.2 %reduce-scatter.2.cloned.1.call-done = bf16[16,8192]{1,0:T(8,128)(2,1)} async-done(((bf16[256,8192]{1,0:T(8,128)(2,1)}), bf16[16,8192]{1,0:T(8,128)(2,1)}) %reduce-scatter.2.cloned.1.call-update) | async-done | bytes 262160 | tf_op jit(solution)/shard_map/reduce_scatter | solution.py:20
  229.2 54.5 %all-reduce.1 = f32[16,8192]{1,0:T(8,128)S(1)} all-reduce(bf16[16,8192]{1,0:T(8,128)(2,1)} %reduce-scatter.2.cloned.1.call-done), channel_id=1, replica_groups=mesh['replica'=16,'shard'=16] {'replica'}, use_global_device_ids=true, to_apply=%region_1.0 | all-reduce | flops 131072 | bytes 786432 | tf_op jit(solution)/shard_map/psum | solution.py:26
  283.7 0.0 copy-done.2
  283.7 0.0 copy-done.1
  283.7 0.0 copy-done
  283.7 1.5 fusion.1
  285.2 0.0 all-gather.2.cloned.1.call-update
  285.2 99.6 %all-gather.2.cloned.1.call-done = bf16[256,8192]{1,0:T(8,128)(2,1)} async-done(((bf16[16,8192]{1,0:T(8,128)(2,1)}), bf16[256,8192]{1,0:T(8,128)(2,1)}) %all-gather.2.cloned.1.call-update) | async-done | bytes 4194320 | tf_op jit(solution)/shard_map/all_gather | solution.py:28
  384.8 4.6 %copy.11 = bf16[256,8192]{1,0:T(8,128)(2,1)} copy(bf16[256,8192]{1,0:T(8,128)(2,1)} %all-gather.2.cloned.1.call-done) | data formatting | bytes 8388608
Async XLA Ops:
  7.2 276.5 %copy-start.2 = (f32[16,8192]{1,0:T(8,128)S(1)}, f32[16,8192]{1,0:T(8,128)}, u32[]{:S(2)}) copy-start(f32[16,8192]{1,0:T(8,128)} %param.7) | copy-start | bytes 1572868
  7.2 276.5 %copy-start.1 = (f32[16,8192]{1,0:T(8,128)S(1)}, f32[16,8192]{1,0:T(8,128)}, u32[]{:S(2)}) copy-start(f32[16,8192]{1,0:T(8,128)} %param.6) | copy-start | bytes 1572868
  7.2 276.5 %copy-start = (f32[16,8192]{1,0:T(8,128)S(1)}, f32[16,8192]{1,0:T(8,128)}, u32[]{:S(2)}) copy-start(f32[16,8192]{1,0:T(8,128)} %param.5) | copy-start | bytes 1572868
  7.2 222.0 %reduce-scatter.2.cloned.1.call-start = ((), (), s32[]{:S(2)}) async-start(), calls=%async_computation.1 | async-start | bytes 4456448 | tf_op jit(solution)/shard_map/reduce_scatter | solution.py:20
  7.9 376.8 %all-gather.2.cloned.1.call-start = ((), (), s32[]{:S(2)}) async-start(), calls=%async_computation.2 | async-start | bytes 4456448 | tf_op jit(solution)/shard_map/all_gather | solution.py:28
Sparse Core Ops, SparseCore 0:
  12.0 217.1 reduce-scatter.1
  285.3 99.4 all-gather.1
where the time goes:
time: 397 us; the launch traced here: 396 us
  waiting for transfers between devices  321 us (81%)
  blocking collectives  54.5 us (14%)
  between operations  14.1 us (4%)
  local copies, waits for them, and re-layouts  4.65 us (1%)
    reduce_scatter x1, waiting for transfers between devices, local(): lax.psum_scatter(local_grad.astype(jnp.float32).astype(jnp.bfloat16), 'sh...  221 us
    all_gather x1, waiting for transfers between devices, local(): lax.all_gather(updated.astype(jnp.bfloat16), 'shard', axis=0, tiled=True)  99.6 us
    psum x1, blocking collectives, local(): total = lax.psum(group_sum, 'replica')  54.5 us
  transfers between devices with their start and end apart: 2, of which 2 were waited for; matrix products, arithmetic and copies ran while one was open for 0% of the time, Pallas kernels for 0%

commit v1 on v0

--- a/solution.py
+++ b/solution.py
@@ -23,7 +23,7 @@
         scatter_dimension=0,
         tiled=True,
     ).astype(jnp.float32)
-    total = lax.psum(group_sum, "replica")
+    total = jnp.sum(lax.all_gather(group_sum, "replica"), axis=0)
     updated, first, second = adam_update(total, master, moment_one, moment_two)
     weights = lax.all_gather(updated.astype(jnp.bfloat16), "shard", axis=0, tiled=True)
     return (updated, first, second, weights)

time: 397 us -> 402 us (1.013)
  waiting for transfers between devices: 321 us -> 376 us
  blocking collectives: 54.5 us -> 0 us
  other arithmetic: 1.47 us -> 7.18 us
    psum x1 -> x0, blocking collectives: 54.5 us -> none  [local(): total = lax.psum(group_sum, 'replica')]
    all_gather x0 -> x1, waiting for transfers between devices: none -> 53 us  [local(): total = jnp.sum(lax.all_gather(group_sum, 'replica'), axis=0)]
  transfers between devices with their start and end apart: 2 -> 3, of which waited for: 2 -> 3; matrix products, arithmetic and copies ran while one was open for 0% -> 0% of each run, Pallas kernels for 0% -> 0%
where the time goes in v1:
time: 402 us
  waiting for transfers between devices  376 us (94%)
  between operations  13.8 us (3%)
  other arithmetic  7.18 us (2%)
  local copies, waits for them, and re-layouts  4.65 us (1%)
    reduce_scatter x1, waiting for transfers between devices, local(): lax.psum_scatter(local_grad.astype(jnp.float32).astype(jnp.bfloat16), 'sh...  221 us
    all_gather x1, waiting for transfers between devices, local(): lax.all_gather(updated.astype(jnp.bfloat16), 'shard', axis=0, tiled=True)  101 us
    all_gather x1, waiting for transfers between devices, local(): total = jnp.sum(lax.all_gather(group_sum, 'replica'), axis=0)  53 us
  transfers between devices with their start and end apart: 3, of which 3 were waited for; matrix products, arithmetic and copies ran while one was open for 0% of the time, Pallas kernels for 0%

profile of v1, /device:TPU:2, one launch (start us, length us, event | category | flops | bytes accessed | tf_op | source)
XLA Modules:
  0.0 401.6 jit_solution(6137524616271892713)
XLA Ops:
  7.2 0.0 reduce-scatter.2.cloned.1.call-start
  7.2 0.7 reduce-scatter.2.cloned.1.call-update
  7.9 0.0 all-gather.6.cloned.1.call-start
  7.9 221.2 %reduce-scatter.2.cloned.1.call-done = bf16[16,8192]{1,0:T(8,128)(2,1)} async-done(((bf16[256,8192]{1,0:T(8,128)(2,1)}), bf16[16,8192]{1,0:T(8,128)(2,1)}) %reduce-scatter.2.cloned.1.call-update) | async-done | bytes 262160 | tf_op jit(solution)/shard_map/reduce_scatter | solution.py:20
  229.2 1.8 all_gather.16
  230.9 0.0 all-gather.6.cloned.1.call-update
  231.0 0.0 all-gather.4.cloned.1.call-start
  231.0 53.0 %all-gather.6.cloned.1.call-done = f32[256,8192]{1,0:T(8,128)} async-done(((f32[16,8192]{1,0:T(8,128)}), f32[256,8192]{1,0:T(8,128)}) %all-gather.6.cloned.1.call-update) | async-done | bytes 8388624 | tf_op jit(solution)/shard_map/all_gather | solution.py:26
  284.0 0.0 copy-start
  284.0 0.0 copy-start.1
  284.0 0.0 copy-start.2
  284.0 3.9 reduce_sum.9
  288.0 0.0 copy-done
  288.0 0.0 copy-done.1
  288.0 0.0 copy-done.2
  288.0 1.5 fusion.1
  289.5 0.0 all-gather.4.cloned.1.call-update
  289.5 100.9 %all-gather.4.cloned.1.call-done = bf16[256,8192]{1,0:T(8,128)(2,1)} async-done(((bf16[16,8192]{1,0:T(8,128)(2,1)}), bf16[256,8192]{1,0:T(8,128)(2,1)}) %all-gather.4.cloned.1.call-update) | async-done | bytes 4194320 | tf_op jit(solution)/shard_map/all_gather | solution.py:28
  390.4 4.6 %copy.9 = bf16[256,8192]{1,0:T(8,128)(2,1)} copy(bf16[256,8192]{1,0:T(8,128)(2,1)} %all-gather.4.cloned.1.call-done) | data formatting | bytes 8388608
Async XLA Ops:
  7.2 222.0 %reduce-scatter.2.cloned.1.call-start = ((), (), s32[]{:S(2)}) async-start(), calls=%async_computation.1 | async-start | bytes 4456448 | tf_op jit(solution)/shard_map/reduce_scatter | solution.py:20
  7.9 276.1 %all-gather.6.cloned.1.call-start = ((), (), s32[]{:S(2)}) async-start(), calls=%async_computation.3 | async-start | bytes 8912896 | tf_op jit(solution)/shard_map/all_gather | solution.py:26
  231.0 159.5 %all-gather.4.cloned.1.call-start = ((), (), s32[]{:S(2)}) async-start(), calls=%async_computation.2 | async-start | bytes 4456448 | tf_op jit(solution)/shard_map/all_gather | solution.py:28
  284.0 3.9 copy-start
  284.0 4.0 copy-start.1
  284.0 4.0 copy-start.2
Sparse Core Ops, SparseCore 0:
  12.0 217.1 reduce-scatter.1
  231.6 52.4 all-gather.5
  289.6 100.7 all-gather.3
